TPU v7x, 256 devices: a whole 4x4x8 slice. The times are simulated.
256 devices in a mesh: users: 64 (over x, z, y_hi), items: 4 (over y_lo, core).
Axes of the slice: x: 4, y: 4 (y_hi: 2, y_lo: 2; y = y_hi * 2 + y_lo), z: 8, core: 2. Of those that a mesh axis runs over, the one named last changes fastest.
Arguments:
- user_factors: bfloat16 [131072, 128], P('users'), may hold values from -0.5 to 0.5
- item_factors: float32 [4, 4, 512, 128], P('items', None, 'users'), may hold values from -6 to 6
- tile_user: int32 [64, 4, 4, 16], P('users', 'items'), may hold values from 0 to 7, as said below
- tile_item: int32 [64, 4, 4, 16], P('users', 'items'), may hold values from 0 to 1, as said below
- tile_count: int32 [64, 4, 4], P('users', 'items'), may hold values from 1 to 16, as said below
- ratings: bfloat16 [64, 4, 4, 16, 256, 256], P('users', 'items'), may hold values from -6 to 6
- mask: int32 [64, 4, 4, 16, 32, 256], P('users', 'items'), may hold values from 0 to 255
Outputs:
- new_items: float32 [4, 4, 512, 128], P('items', None, 'users')
- user_grad: float32 [131072, 128], P(('users', 'items'))
Inputs may be any that keep to these rules, and one draw needn't show every extreme that they name: `tile_user`: index of a user tile within its user block. `tile_item`: index of an item tile within its panel; the pairs (tile_user, tile_item) of one user block, owner and panel are distinct. Only the first tile_count slots of a user block, owner and panel hold observed tiles; the other slots are to be ignored. For every owner and panel some user block fills all 16 slots. Bit k of word mask[..., w, j] marks the rating in row 8 * w + k, column j of the tile as observed.
All inputs are finite; a program needn't handle non-finite values.
Results may differ from a plain program's by a relative error of at most 0.0031.
Values may be sent and summed in bfloat16 or wider, within the bound.
A program may use at most 128 MiB of HBM per device.

v0:
```python
import math

import jax
import jax.numpy as jnp
from jax import lax
from jax.sharding import PartitionSpec as P


def shards(user_factors, item_factors, tile_user, tile_item, tile_count, ratings, mask):
    users_count = lax.axis_size("users")
    rank_width = user_factors.shape[1]
    tile_side = ratings.shape[-1]
    user_tiles = user_factors.shape[0] // tile_side
    step_count = item_factors.shape[1]
    slot_count = ratings.shape[3]
    local_rows = item_factors.shape[2]
    panel_rows = local_rows * users_count
    panel_tiles = panel_rows // tile_side
    user_blocks = user_factors.reshape(user_tiles, tile_side, rank_width)
    step_rate = 8.0 / math.sqrt(tile_side * users_count)
    shifts = jnp.arange(8, dtype=jnp.int32)
    user_sum = jnp.zeros((user_tiles, tile_side, rank_width), jnp.float32)
    updated = []
    for step_index in range(step_count):
        panel_bf = lax.all_gather(
            item_factors[0, step_index].astype(jnp.bfloat16), "users", axis=0, tiled=True
        )
        tiles_of_panel = panel_bf.reshape(panel_tiles, tile_side, rank_width)
        user_index = tile_user[0, 0, step_index]
        item_index = tile_item[0, 0, step_index]
        user_rows = user_blocks[user_index]
        item_rows = tiles_of_panel[item_index]
        predicted = jnp.einsum(
            "tir,tjr->tij", user_rows, item_rows, preferred_element_type=jnp.float32
        )
        mask_bits = mask[0, 0, step_index][:, :, None, :] >> shifts[None, None, :, None] & 1
        observed = mask_bits.reshape(slot_count, tile_side, tile_side).astype(jnp.float32)
        live_slots = (jnp.arange(slot_count) < tile_count[0, 0, step_index]).astype(jnp.float32)
        errors = (
            observed
            * live_slots[:, None, None]
            * (predicted - ratings[0, 0, step_index].astype(jnp.float32))
        ).astype(jnp.bfloat16)
        tile_grad = jnp.einsum(
            "tij,tir->tjr", errors, user_rows, preferred_element_type=jnp.float32
        )
        item_onehot = (
            item_index[:, None] == jnp.arange(panel_tiles, dtype=jnp.int32)[None, :]
        ).astype(jnp.float32)
        panel_grad = jnp.einsum(
            "tp,tjr->pjr", item_onehot, tile_grad, precision=lax.Precision.HIGHEST
        ).reshape(panel_rows, rank_width)
        user_part = jnp.einsum(
            "tij,tjr->tir", errors, item_rows, preferred_element_type=jnp.float32
        )
        user_onehot = (
            user_index[:, None] == jnp.arange(user_tiles, dtype=jnp.int32)[None, :]
        ).astype(jnp.float32)
        user_sum = user_sum + jnp.einsum(
            "tu,tir->uir", user_onehot, user_part, precision=lax.Precision.HIGHEST
        )
        whole_sum = lax.psum(panel_grad, "users")
        own_rows = lax.dynamic_slice_in_dim(
            whole_sum, lax.axis_index("users") * local_rows, local_rows, 0
        )
        updated.append(0.95 * item_factors[0, step_index] - step_rate * own_rows)
    new_items = jnp.stack(updated)[None]
    user_terms = user_sum.reshape(user_tiles * tile_side, rank_width) / 32.0
    user_grad = lax.psum_scatter(user_terms, "items", scatter_dimension=0, tiled=True)
    return (new_items, user_grad)


def solution(mesh):
    return jax.shard_map(
        shards,
        mesh=mesh,
        in_specs=(
            P("users", None),
            P("items", None, "users", None),
            P("users", "items", None, None),
            P("users", "items", None, None),
            P("users", "items", None),
            P("users", "items", None, None, None, None),
            P("users", "items", None, None, None, None),
        ),
        out_specs=(P("items", None, "users", None), P(("users", "items"), None)),
        check_vma=False,
    )
```

profile of v0, /device:TPU:8, one launch (start us, length us, event | category | flops | bytes accessed | tf_op | source)
XLA Modules:
  0.0 1480.3 jit_solution(12672225782933500393)
XLA Ops:
  8.1 1.5 fusion.89
  9.5 1.2 compare_convert_fusion.3
  10.7 1.2 compare_convert_fusion.2
  13.0 1.3 compare_convert_fusion.1
  14.3 1.4 slice_bitcast_fusion.11
  18.0 184.3 %all-gather = bf16[1,1,512,128]{3,2,1,0:T(8,128)(2,1)S(1)} all-gather(bf16[1,1,8,128]{3,2,1,0:T(8,128)(2,1)S(1)} %get-tuple-element.14), channel_id=2, replica_groups=mesh['users'=64,'items'=4] {'users'}, dimensions={2}, use_global_device_ids=true | all-gather | bytes 133120 | tf_op jit(solution)/shard_map/all_gather | solution.py:25
  202.4 174.5 %all-gather.1 = bf16[1,1,512,128]{3,2,1,0:T(8,128)(2,1)S(1)} all-gather(bf16[1,1,8,128]{3,2,1,0:T(8,128)(2,1)S(1)} %get-tuple-element.15), channel_id=3, replica_groups=mesh['users'=64,'items'=4] {'users'}, dimensions={2}, use_global_device_ids=true | all-gather | bytes 133120 | tf_op jit(solution)/shard_map/all_gather | solution.py:25
  376.9 178.1 %all-gather.2 = bf16[1,1,512,128]{3,2,1,0:T(8,128)(2,1)S(1)} all-gather(bf16[1,1,8,128]{3,2,1,0:T(8,128)(2,1)S(1)} %get-tuple-element.16), channel_id=4, replica_groups=mesh['users'=64,'items'=4] {'users'}, dimensions={2}, use_global_device_ids=true | all-gather | bytes 133120 | tf_op jit(solution)/shard_map/all_gather | solution.py:25
  555.0 174.5 %all-gather.3 = bf16[1,1,512,128]{3,2,1,0:T(8,128)(2,1)S(1)} all-gather(bf16[1,1,8,128]{3,2,1,0:T(8,128)(2,1)S(1)} %get-tuple-element.17), channel_id=5, replica_groups=mesh['users'=64,'items'=4] {'users'}, dimensions={2}, use_global_device_ids=true | all-gather | bytes 133120 | tf_op jit(solution)/shard_map/all_gather | solution.py:25
  729.5 1.7 gather_fusion.4
  731.2 1.7 gather_fusion.6
  732.8 1.7 gather_fusion.2
  734.5 1.6 gather_fusion
  736.2 2.7 slice_bitcast_fusion.3
  738.9 1.6 gather_fusion.1
  740.5 3.5 fusion.7
  744.9 2.0 fusion.34
  747.6 1.8 gather_fusion.3
  749.3 3.5 fusion.5
  754.2 2.0 fusion.32
  757.0 1.7 gather_fusion.7
  758.7 3.5 fusion.1
  763.5 2.1 fusion.28
  766.4 1.7 gather_fusion.5
  768.1 3.4 fusion.3
  772.9 2.0 fusion.30
  775.7 2.7 fusion.95
  781.1 2.0 fusion.24
  783.1 2.0 fusion.20
  785.0 2.0 fusion.22
  787.8 2.2 fusion.45
  791.2 680.4 %all-reduce.3.cloned.1.call-done = (f32[512,128]{1,0:T(8,128)}, f32[512,128]{1,0:T(8,128)}, f32[512,128]{1,0:T(8,128)}, f32[512,128]{1,0:T(8,128)}) async-done(((f32[512,128]{1,0:T(8,128)}, f32[512,128]{1,0:T(8,128)}, f32[512,128]{1,0:T(8,128)}, f32[512,128]{1,0:T(8,128)}), (f32[512,128]{1,0:T(8,128)}, f32[512,128]{1,0:T(8,128)}, f32[512,128]{1,0:T(8,128)}, ...) | async-done | bytes 1048592 | tf_op jit(solution)/shard_map/psum | solution.py:62
  (75 shorter events, 17.0 us)
Async XLA Ops:
  8.0 721.5 %copy-start = (bf16[2048,128]{1,0:T(8,128)(2,1)S(1)}, bf16[2048,128]{1,0:T(8,128)(2,1)}, u32[]{:S(2)}) copy-start(bf16[2048,128]{1,0:T(8,128)(2,1)} %param.7) | copy-start | bytes 1572868
  8.0 1463.5 %all-reduce.3.cloned.1.call-start = ((), (), s32[]{:S(2)}) async-start(), calls=%async_computation.2 | async-start | bytes 2097152 | tf_op jit(solution)/shard_map/psum | solution.py:62
  740.5 3.6 copy-start.12
  744.1 0.8 copy-start.17
  749.3 3.5 copy-start.11
  752.9 1.4 copy-start.1
  752.9 1.3 copy-start.16
  754.2 4.4 copy-start.18
  754.2 4.4 copy-start.20
  758.7 3.5 copy-start.9
  762.2 1.3 copy-start.2
  762.2 1.3 copy-start.15
  763.5 4.5 copy-start.19
  768.1 3.5 copy-start.7
  771.5 1.4 copy-start.4
  772.9 2.8 copy-start.14
  775.6 697.2 %reduce-scatter.2.cloned.1.call-start = ((), (), s32[]{:S(2)}) async-start(), calls=%async_computation.1 | async-start | bytes 1310720 | tf_op jit(solution)/shard_map/reduce_scatter | solution.py:69
  775.7 2.7 copy-start.3
  775.7 2.8 copy-start.8
  778.5 1.6 copy-start.5
  778.5 1.9 copy-start.10
  785.0 2.0 copy-start.6
  790.0 681.6 %copy-start.13 = (f32[1,4,8,128]{3,2,1,0:T(8,128)S(1)}, f32[1,4,8,128]{3,2,1,0:T(8,128)}, u32[]{:S(2)}) copy-start(f32[1,4,8,128]{3,2,1,0:T(8,128)} %param.8) | copy-start | bytes 49156
Sparse Core Ops, SparseCore 0:
  775.8 695.7 all-reduce.2
Sparse Core Ops, SparseCore 1:
  791.3 17.1 reduce-scatter.1
where the time goes:
time: 1480 us
  blocking collectives  711 us (48%)
  waiting for transfers between devices  680 us (46%)
  matrix products  38.1 us (3%)
  local copies, waits for them, and re-layouts  27.5 us (2%)
  between operations  15.9 us (1%)
    all_gather x4, blocking collectives, shards(): lax.all_gather(item_factors[0, step_index].astype(jnp.bfloat16), 'users',...  711 us
    psum x1, waiting for transfers between devices, shards(): whole_sum = lax.psum(panel_grad, 'users')  680 us
  transfers between devices with their start and end apart: 2, of which 1 were waited for; matrix products, arithmetic and copies ran while one was open for 1% of the time, Pallas kernels for 0%

commit v1 on v0

v1 whole, which is shorter than its diff:
```python
import functools
import math

import jax
import jax.numpy as jnp
from jax import lax
from jax.experimental import pallas as pl
from jax.experimental.pallas import tpu as pltpu
from jax.sharding import PartitionSpec as P

MESH = pl.DeviceIdType.MESH
XS, ZS, YS = 4, 8, 2
ITEMS = 4
STEPS = 4
SLOTS = 16
TILE = 256
UTILES = 8
RANK = 128
ROWS = 8
QROWS = 128
ZY = ZS * YS
F32, BF16 = jnp.float32, jnp.bfloat16


def kernel(
    tile_user, tile_item, tile_count, items, factors, ratings, mask,
    new_items, user_grad,
    slots, lives, cells, rat_v, mask_v, uf, uft, panel, other, err, gacc,
    own_grad, grad_out, grad_in, sums, zy_out, zy_in, user_sum, user_out, user_in,
    load_sem, y_sem, zs_sem, zr_sem, xs_sem, xr_sem, gs_sem, gr_sem,
    zys_sem, zyr_sem, us_sem, ur_sem,
):
    me = lax.axis_index("users")
    it = lax.axis_index("items")
    xi = lax.div(me, ZY)
    zy = lax.rem(me, ZY)
    zi = lax.div(zy, YS)
    yi = lax.rem(zy, YS)

    def at_users(x, z, y):
        return {"users": x * ZY + z * YS + y}

    def ring(value, step, size):
        return lax.rem(value + step, size)

    loads = [pltpu.make_async_copy(factors, uf, load_sem.at[16])]
    for s in range(STEPS):
        for half in range(2):
            lanes = pl.ds(half * 128, 128)
            rows = pl.ds(s * SLOTS, SLOTS)
            loads.append(pltpu.make_async_copy(
                mask.at[0, 0, s, :, :, lanes], mask_v.at[half, rows], load_sem.at[s * 2 + half]))
            loads.append(pltpu.make_async_copy(
                ratings.at[0, 0, s, :, :, lanes], rat_v.at[half, rows], load_sem.at[8 + s * 2 + half]))

    barrier = pltpu.get_barrier_semaphore()
    greeted = 0
    for d in range(1, ZY):
        pl.semaphore_signal(barrier, inc=1, device_id={"users": xi * ZY + ring(zy, d, ZY)}, device_id_type=MESH)
        greeted += 1
    for d in range(1, XS):
        pl.semaphore_signal(barrier, inc=1, device_id={"users": ring(xi, d, XS) * ZY + zy}, device_id_type=MESH)
        greeted += 1
    for d in range(1, ITEMS):
        pl.semaphore_signal(barrier, inc=1, device_id={"items": ring(it, d, ITEMS)}, device_id_type=MESH)
        greeted += 1
    for load in loads:
        load.start()
    pl.semaphore_wait(barrier, greeted)

    y_copy = pltpu.make_async_remote_copy(
        src_ref=items.at[0], dst_ref=other, send_sem=y_sem.at[0], recv_sem=y_sem.at[1],
        device_id=at_users(xi, zi, 1 - yi), device_id_type=MESH)
    y_copy.start()

    for s in range(STEPS):
        for t in range(SLOTS):
            cell = tile_user[0, 0, s, t] * 2 + tile_item[0, 0, s, t]
            cells[s * SLOTS + t] = jnp.where(t < tile_count[0, 0, s], cell, -1)

    @pl.loop(0, STEPS * SLOTS)
    def _(idx):
        first = lax.div(idx, SLOTS) * SLOTS
        cell = lax.rem(idx, SLOTS)
        slot = jnp.int32(0)
        live = jnp.int32(0)
        for t in range(SLOTS):
            hit = cells[first + t] == cell
            slot = jnp.where(hit, t, slot)
            live = jnp.where(hit, -1, live)
        slots[idx] = slot
        lives[idx] = live

    user_sum[...] = jnp.zeros_like(user_sum)

    y_copy.wait_recv()
    mine = items[0]
    theirs = other[...]
    low = jnp.where(yi == 0, mine, theirs)
    high = jnp.where(yi == 0, theirs, mine)
    my_rows = pl.ds(pl.multiple_of(zi * 16, 16), 16)
    panel[xi, :, my_rows, :] = jnp.concatenate([low, high], axis=1).astype(BF16)

    z_copies = []
    for d in (4, 3, 5, 2, 6, 1, 7):
        part = panel.at[xi, :, my_rows, :]
        copy = pltpu.make_async_remote_copy(
            src_ref=part, dst_ref=part, send_sem=zs_sem.at[d], recv_sem=zr_sem.at[d],
            device_id=at_users(xi, ring(zi, d, ZS), yi), device_id_type=MESH)
        copy.start()
        z_copies.append(copy)

    for load in loads:
        load.wait()
    uft[...] = uf[...].T

    for copy in z_copies:
        copy.wait_recv()

    def x_copy(h, d):
        part = panel.at[xi, pl.ds(2 * h, 2)]
        return pltpu.make_async_remote_copy(
            src_ref=part, dst_ref=part, send_sem=xs_sem.at[h, d], recv_sem=xr_sem.at[h, d],
            device_id=at_users(ring(xi, d, XS), zi, yi), device_id_type=MESH)

    for h in range(2):
        for d in (1, 3, 2):
            x_copy(h, d).start()

    bits = jnp.left_shift(jnp.int32(1), lax.broadcasted_iota(jnp.int32, (1, 8, 128), 1))

    def g_copy(h, d):
        return pltpu.make_async_remote_copy(
            src_ref=grad_out.at[h, d], dst_ref=grad_in.at[h, d],
            send_sem=gs_sem.at[h, d], recv_sem=gr_sem.at[h, d],
            device_id=at_users(ring(xi, d, XS), zi, yi), device_id_type=MESH)

    def chunk(q, h):
        pair = panel[q, pl.ds(2 * h, 2)].reshape(2 * QROWS, RANK)
        half = lax.rem(q, 2)
        p = lax.div(q, 2)
        for u in range(UTILES):
            span = pl.ds(u * TILE, TILE)
            predicted = lax.dot_general(
                uf[span, :], pair, (((1,), (1,)), ((), ())), preferred_element_type=F32)
            parts = []
            for k in range(2):
                first = (2 * h + k) * SLOTS
                slot = first + slots[first + 2 * u + p]
                live = lives[first + 2 * u + p]
                words = mask_v[half, slot] & live
                seen = (jnp.broadcast_to(words[:, None, :], (32, 8, 128)) & bits) != 0
                gap = predicted[:, k * 128:(k + 1) * 128] - rat_v[half, slot].astype(F32)
                kept = jnp.where(seen, gap.reshape(32, 8, 128), 0.0)
                parts.append(kept.reshape(TILE, 128).astype(BF16))
            errors = jnp.concatenate(parts, axis=1)
            err[span, :] = errors
            user_sum[span, :] += jnp.dot(errors, pair, preferred_element_type=F32)
        gacc[...] = jnp.dot(uft[...], err[...], preferred_element_type=F32)
        return gacc[...].T.reshape(2, QROWS, RANK)

    @pl.loop(0, 8)
    def _(c):
        h = lax.div(c, 4)
        k = lax.rem(c, 4)
        d = jnp.where(h == 0, jnp.where(k == 3, 2, jnp.where(k == 2, 3, k)),
                      jnp.where(k == 3, 0, jnp.where(k == 2, 3, 2 - k)))
        q = ring(xi, d, XS)

        @pl.when(d != 0)
        def _():
            x_copy(h, XS - d).wait_recv()

        grad = chunk(q, h)

        @pl.when(d == 0)
        def _():
            own_grad[h] = grad

        @pl.when(d != 0)
        def _():
            grad_out[h, d] = grad.astype(BF16)
            g_copy(h, d).start()

    def u_copy(d):
        return pltpu.make_async_remote_copy(
            src_ref=user_out.at[d], dst_ref=user_in.at[d],
            send_sem=us_sem.at[d], recv_sem=ur_sem.at[d],
            device_id={"items": ring(it, d, ITEMS)}, device_id_type=MESH)

    share = 2 * TILE
    for d in (2, 3, 1):
        rows = pl.ds(pl.multiple_of(ring(it, d, ITEMS) * share, share), share)
        user_out[d] = user_sum[rows, :].astype(BF16)
        u_copy(d).start()

    def zy_copy(h, d):
        return pltpu.make_async_remote_copy(
            src_ref=zy_out.at[h, d], dst_ref=zy_in.at[h, d],
            send_sem=zys_sem.at[h, d], recv_sem=zyr_sem.at[h, d],
            device_id={"users": xi * ZY + ring(zy, d, ZY)}, device_id_type=MESH)

    for h in range(2):
        for d in range(1, XS):
            g_copy(h, d).wait_recv()
        sums[h] = own_grad[h] + (
            grad_in[h, 1].astype(F32) + grad_in[h, 2].astype(F32) + grad_in[h, 3].astype(F32))
        for d in range(1, ZY):
            rows = pl.ds(pl.multiple_of(ring(zy, d, ZY) * ROWS, ROWS), ROWS)
            zy_out[h, d] = sums[h, :, rows, :].reshape(2 * ROWS, RANK).astype(BF16)
        for d in (8, 7, 9, 6, 10, 5, 11, 4, 12, 3, 13, 2, 14, 1, 15):
            zy_copy(h, d).start()

    my_share = pl.ds(pl.multiple_of(it * share, share), share)
    for d in range(1, ITEMS):
        u_copy(d).wait_recv()
    user_grad[...] = (user_sum[my_share, :] + (
        user_in[1].astype(F32) + user_in[2].astype(F32) + user_in[3].astype(F32))) * (1.0 / 32.0)

    step_rate = 8.0 / math.sqrt(TILE * XS * ZY)
    mine_rows = pl.ds(pl.multiple_of(zy * ROWS, ROWS), ROWS)
    for h in range(2):
        total = sums[h, :, mine_rows, :].reshape(2 * ROWS, RANK)
        for d in range(1, ZY):
            zy_copy(h, d).wait_recv()
            total = total + zy_in[h, d].astype(F32)
        pair = pl.ds(2 * h, 2)
        new_items[0, pair] = 0.95 * items[0, pair] - step_rate * total.reshape(2, ROWS, RANK)

    y_copy.wait_send()
    for copy in z_copies:
        copy.wait_send()
    for h in range(2):
        for d in range(1, XS):
            x_copy(h, d).wait_send()
            g_copy(h, d).wait_send()
        for d in range(1, ZY):
            zy_copy(h, d).wait_send()
    for d in range(1, ITEMS):
        u_copy(d).wait_send()


def shards(user_factors, item_factors, tile_user, tile_item, tile_count, ratings, mask):
    smem = pl.BlockSpec(memory_space=pltpu.SMEM)
    vmem = pl.BlockSpec(memory_space=pltpu.VMEM)
    hbm = pl.BlockSpec(memory_space=pl.ANY)
    dma = pltpu.SemaphoreType.DMA
    return pl.pallas_call(
        kernel,
        out_shape=(
            jax.ShapeDtypeStruct(item_factors.shape, F32),
            jax.ShapeDtypeStruct((user_factors.shape[0] // ITEMS, RANK), F32),
        ),
        in_specs=[smem, smem, smem, vmem, hbm, hbm, hbm],
        out_specs=(vmem, vmem),
        scratch_shapes=[
            pltpu.SMEM((STEPS * SLOTS,), jnp.int32),
            pltpu.SMEM((STEPS * SLOTS,), jnp.int32),
            pltpu.SMEM((STEPS * SLOTS,), jnp.int32),
            pltpu.VMEM((2, STEPS * SLOTS, TILE, 128), BF16),
            pltpu.VMEM((2, STEPS * SLOTS, TILE // 8, 128), jnp.int32),
            pltpu.VMEM((UTILES * TILE, RANK), BF16),
            pltpu.VMEM((RANK, UTILES * TILE), BF16),
            pltpu.VMEM((XS, STEPS, QROWS, RANK), BF16),
            pltpu.VMEM((STEPS, ROWS, RANK), F32),
            pltpu.VMEM((UTILES * TILE, 2 * QROWS), BF16),
            pltpu.VMEM((RANK, 2 * QROWS), F32),
            pltpu.VMEM((2, 2, QROWS, RANK), F32),
            pltpu.VMEM((2, XS, 2, QROWS, RANK), BF16),
            pltpu.VMEM((2, XS, 2, QROWS, RANK), BF16),
            pltpu.VMEM((2, 2, QROWS, RANK), F32),
            pltpu.VMEM((2, ZY, 2 * ROWS, RANK), BF16),
            pltpu.VMEM((2, ZY, 2 * ROWS, RANK), BF16),
            pltpu.VMEM((UTILES * TILE, RANK), F32),
            pltpu.VMEM((ITEMS, 2 * TILE, RANK), BF16),
            pltpu.VMEM((ITEMS, 2 * TILE, RANK), BF16),
            dma((17,)), dma((2,)), dma((ZS,)), dma((ZS,)),
            dma((2, XS)), dma((2, XS)), dma((2, XS)), dma((2, XS)),
            dma((2, ZY)), dma((2, ZY)), dma((ITEMS,)), dma((ITEMS,)),
        ],
        compiler_params=pltpu.CompilerParams(
            collective_id=0, has_side_effects=True, vmem_limit_bytes=40 * 2**20),
        name="factor_step",
    )(tile_user, tile_item, tile_count, item_factors, user_factors, ratings, mask)


def solution(mesh):
    return jax.shard_map(
        shards,
        mesh=mesh,
        in_specs=(
            P("users", None),
            P("items", None, "users", None),
            P("users", "items", None, None),
            P("users", "items", None, None),
            P("users", "items", None),
            P("users", "items", None, None, None, None),
            P("users", "items", None, None, None, None),
        ),
        out_specs=(P("items", None, "users", None), P(("users", "items"), None)),
        check_vma=False,
    )
```

time: 1480 us -> 51.9 us (0.04)
  the two profiles are of different devices: /device:TPU:8 before, /device:TPU:6 now
where the time goes in v1:
time: 51.9 us; the launch traced here: 51.6 us
  Pallas kernels  40.9 us (79%)
  local copies, waits for them, and re-layouts  10 us (19%)
  between operations  0.66 us (1%)
    pallas_call x1, Pallas kernels, shards(): pl.pallas_call(kernel, out_shape=(jax.ShapeDtypeStruct(item_factors.shape...  40.9 us
    unnamed x16, local copies, waits for them, and re-layouts  10 us

profile of v1, /device:TPU:6, one launch (start us, length us, event | category | flops | bytes accessed | tf_op | source)
XLA Modules:
  0.0 51.6 jit_solution(4617807729315254138)
XLA Ops:
  0.6 0.0 copy-start
  0.6 3.4 %copy-done = bf16[1,1,4,16,256,256]{5,4,3,2,1,0:T(8,128)(2,1)S(1)} copy-done((bf16[1,1,4,16,256,256]{5,4,3,2,1,0:T(8,128)(2,1)S(1)}, bf16[1,1,4,16,256,256]{5,4,3,2,1,0:T(8,128)(2,1)}, u32[]{:S(2)}) %copy-start) | copy-done | bytes 8388632
  4.0 0.0 copy-start.1
  4.0 1.6 %copy-done.1 = s32[1,1,4,16,32,256]{5,4,3,2,1,0:T(8,128)S(1)} copy-done((s32[1,1,4,16,32,256]{5,4,3,2,1,0:T(8,128)S(1)}, s32[1,1,4,16,32,256]{5,4,3,2,1,0:T(8,128)}, u32[]{:S(2)}) %copy-start.1) | copy-done | bytes 2097176
  5.6 0.0 copy-start.2
  5.6 1.0 %copy-done.2 = bf16[2048,128]{1,0:T(8,128)(2,1)S(1)} copy-done((bf16[2048,128]{1,0:T(8,128)(2,1)S(1)}, bf16[2048,128]{1,0:T(8,128)(2,1)}, u32[]{:S(2)}) %copy-start.2) | copy-done | bytes 524312
  6.6 0.0 copy-start.3
  6.7 0.7 %copy-done.3 = f32[1,4,8,128]{3,2,1,0:T(8,128)S(1)} copy-done((f32[1,4,8,128]{3,2,1,0:T(8,128)S(1)}, f32[1,4,8,128]{3,2,1,0:T(8,128)}, u32[]{:S(2)}) %copy-start.3) | copy-done | bytes 16408
  7.4 0.0 copy-start.4
  7.4 0.7 %copy-done.4 = s32[1,1,4,16]{3,2,1,0:T(4,128)S(1)} copy-done((s32[1,1,4,16]{3,2,1,0:T(4,128)S(1)}, s32[1,1,4,16]{3,2,1,0:T(4,128)}, u32[]{:S(2)}) %copy-start.4) | copy-done | bytes 280
  8.0 0.0 copy-start.5
  8.1 0.7 %copy-done.5 = s32[1,1,4,16]{3,2,1,0:T(4,128)S(1)} copy-done((s32[1,1,4,16]{3,2,1,0:T(4,128)S(1)}, s32[1,1,4,16]{3,2,1,0:T(4,128)}, u32[]{:S(2)}) %copy-start.5) | copy-done | bytes 280
  8.7 0.0 copy-start.6
  8.7 0.7 %copy-done.6 = s32[1,1,4]{2,1,0:T(1,128)S(1)} copy-done((s32[1,1,4]{2,1,0:T(1,128)S(1)}, s32[1,1,4]{2,1,0:T(1,128)}, u32[]{:S(2)}) %copy-start.6) | copy-done | bytes 40
  9.4 40.9 %factor_step.1 = (f32[1,4,8,128]{3,2,1,0:T(8,128)S(1)}, f32[512,128]{1,0:T(8,128)S(1)}) custom-call(s32[1,1,4,16]{3,2,1,0:T(4,128)S(1)} %copy-done.4, s32[1,1,4,16]{3,2,1,0:T(4,128)S(1)} %copy-done.5, s32[1,1,4]{2,1,0:T(1,128)S(1)} %copy-done.6, f32[1,4,8,128]{3,2,1,0:T(8,128)S(1)} %copy-done.3, bf16[2048,128]{1,0:T(8,128)(2,1)S(1)} %copy-done.2, ...), custom_call_target="tpu_custom_call" | custom-call | tf_op jit(solution)/shard_map/factor_step/pallas_call | solution.py:248
  50.3 0.6 %copy.11 = f32[1,4,8,128]{3,2,1,0:T(8,128)} copy(f32[1,4,8,128]{3,2,1,0:T(8,128)S(1)} %get-tuple-element.4) | data formatting | bytes 32768
  50.9 0.7 %copy.12 = f32[512,128]{1,0:T(8,128)} copy(f32[512,128]{1,0:T(8,128)S(1)} %get-tuple-element.5) | data formatting | bytes 524288
Async XLA Ops:
  0.6 3.4 %copy-start = (bf16[1,1,4,16,256,256]{5,4,3,2,1,0:T(8,128)(2,1)S(1)}, bf16[1,1,4,16,256,256]{5,4,3,2,1,0:T(8,128)(2,1)}, u32[]{:S(2)}) copy-start(bf16[1,1,4,16,256,256]{5,4,3,2,1,0:T(8,128)(2,1)} %ratings.1) | copy-start | bytes 25165828
  4.0 1.6 %copy-start.1 = (s32[1,1,4,16,32,256]{5,4,3,2,1,0:T(8,128)S(1)}, s32[1,1,4,16,32,256]{5,4,3,2,1,0:T(8,128)}, u32[]{:S(2)}) copy-start(s32[1,1,4,16,32,256]{5,4,3,2,1,0:T(8,128)} %mask.1) | copy-start | bytes 6291460
  5.6 1.0 %copy-start.2 = (bf16[2048,128]{1,0:T(8,128)(2,1)S(1)}, bf16[2048,128]{1,0:T(8,128)(2,1)}, u32[]{:S(2)}) copy-start(bf16[2048,128]{1,0:T(8,128)(2,1)} %factors.1) | copy-start | bytes 1572868
  6.6 0.7 %copy-start.3 = (f32[1,4,8,128]{3,2,1,0:T(8,128)S(1)}, f32[1,4,8,128]{3,2,1,0:T(8,128)}, u32[]{:S(2)}) copy-start(f32[1,4,8,128]{3,2,1,0:T(8,128)} %items.1) | copy-start | bytes 49156
  7.4 0.7 %copy-start.4 = (s32[1,1,4,16]{3,2,1,0:T(4,128)S(1)}, s32[1,1,4,16]{3,2,1,0:T(4,128)}, u32[]{:S(2)}) copy-start(s32[1,1,4,16]{3,2,1,0:T(4,128)} %tile_user.1) | copy-start | bytes 772
  8.0 0.7 %copy-start.5 = (s32[1,1,4,16]{3,2,1,0:T(4,128)S(1)}, s32[1,1,4,16]{3,2,1,0:T(4,128)}, u32[]{:S(2)}) copy-start(s32[1,1,4,16]{3,2,1,0:T(4,128)} %tile_item.1) | copy-start | bytes 772
  8.7 0.7 %copy-start.6 = (s32[1,1,4]{2,1,0:T(1,128)S(1)}, s32[1,1,4]{2,1,0:T(1,128)}, u32[]{:S(2)}) copy-start(s32[1,1,4]{2,1,0:T(1,128)} %tile_count.1) | copy-start | bytes 52

commit v2 on v1

--- a/solution.py
+++ b/solution.py
@@ -23,8 +23,9 @@
 
 
 def kernel(
-    tile_user, tile_item, tile_count, items, factors, ratings, mask,
+    tile_user_hbm, tile_item_hbm, tile_count_hbm, items_hbm, factors, ratings, mask,
     new_items, user_grad,
+    tile_user, tile_item, tile_count, items,
     slots, lives, cells, rat_v, mask_v, uf, uft, panel, other, err, gacc,
     own_grad, grad_out, grad_in, sums, zy_out, zy_in, user_sum, user_out, user_in,
     load_sem, y_sem, zs_sem, zr_sem, xs_sem, xr_sem, gs_sem, gr_sem,
@@ -43,20 +44,24 @@
     def ring(value, step, size):
         return lax.rem(value + step, size)
 
-    loads = [pltpu.make_async_copy(factors, uf, load_sem.at[16])]
+    tables = [
+        pltpu.make_async_copy(tile_user_hbm, tile_user, load_sem.at[9]),
+        pltpu.make_async_copy(tile_item_hbm, tile_item, load_sem.at[10]),
+        pltpu.make_async_copy(tile_count_hbm, tile_count, load_sem.at[11]),
+        pltpu.make_async_copy(items_hbm, items, load_sem.at[12]),
+    ]
+    loads = [pltpu.make_async_copy(factors, uf, load_sem.at[8])]
     for s in range(STEPS):
-        for half in range(2):
-            lanes = pl.ds(half * 128, 128)
-            rows = pl.ds(s * SLOTS, SLOTS)
-            loads.append(pltpu.make_async_copy(
-                mask.at[0, 0, s, :, :, lanes], mask_v.at[half, rows], load_sem.at[s * 2 + half]))
-            loads.append(pltpu.make_async_copy(
-                ratings.at[0, 0, s, :, :, lanes], rat_v.at[half, rows], load_sem.at[8 + s * 2 + half]))
+        rows = pl.ds(s * SLOTS, SLOTS)
+        loads.append(pltpu.make_async_copy(mask.at[0, 0, s], mask_v.at[rows], load_sem.at[s]))
+        loads.append(pltpu.make_async_copy(ratings.at[0, 0, s], rat_v.at[rows], load_sem.at[4 + s]))
 
     barrier = pltpu.get_barrier_semaphore()
     greeted = 0
-    for d in range(1, ZY):
-        pl.semaphore_signal(barrier, inc=1, device_id={"users": xi * ZY + ring(zy, d, ZY)}, device_id_type=MESH)
+    pl.semaphore_signal(barrier, inc=1, device_id=at_users(xi, zi, 1 - yi), device_id_type=MESH)
+    greeted += 1
+    for d in range(1, ZS):
+        pl.semaphore_signal(barrier, inc=1, device_id=at_users(xi, ring(zi, d, ZS), yi), device_id_type=MESH)
         greeted += 1
     for d in range(1, XS):
         pl.semaphore_signal(barrier, inc=1, device_id={"users": ring(xi, d, XS) * ZY + zy}, device_id_type=MESH)
@@ -64,14 +69,10 @@
     for d in range(1, ITEMS):
         pl.semaphore_signal(barrier, inc=1, device_id={"items": ring(it, d, ITEMS)}, device_id_type=MESH)
         greeted += 1
-    for load in loads:
+    for load in tables + loads:
         load.start()
-    pl.semaphore_wait(barrier, greeted)
-
-    y_copy = pltpu.make_async_remote_copy(
-        src_ref=items.at[0], dst_ref=other, send_sem=y_sem.at[0], recv_sem=y_sem.at[1],
-        device_id=at_users(xi, zi, 1 - yi), device_id_type=MESH)
-    y_copy.start()
+    for load in tables:
+        load.wait()
 
     for s in range(STEPS):
         for t in range(SLOTS):
@@ -93,6 +94,13 @@
 
     user_sum[...] = jnp.zeros_like(user_sum)
 
+    pl.semaphore_wait(barrier, greeted)
+
+    y_copy = pltpu.make_async_remote_copy(
+        src_ref=items_hbm.at[0], dst_ref=other, send_sem=y_sem.at[0], recv_sem=y_sem.at[1],
+        device_id=at_users(xi, zi, 1 - yi), device_id_type=MESH)
+    y_copy.start()
+
     y_copy.wait_recv()
     mine = items[0]
     theirs = other[...]
@@ -101,31 +109,33 @@
     my_rows = pl.ds(pl.multiple_of(zi * 16, 16), 16)
     panel[xi, :, my_rows, :] = jnp.concatenate([low, high], axis=1).astype(BF16)
 
-    z_copies = []
-    for d in (4, 3, 5, 2, 6, 1, 7):
-        part = panel.at[xi, :, my_rows, :]
-        copy = pltpu.make_async_remote_copy(
-            src_ref=part, dst_ref=part, send_sem=zs_sem.at[d], recv_sem=zr_sem.at[d],
+    def z_copy(h, d):
+        part = panel.at[xi, pl.ds(2 * h, 2), my_rows, :]
+        return pltpu.make_async_remote_copy(
+            src_ref=part, dst_ref=part, send_sem=zs_sem.at[h, d], recv_sem=zr_sem.at[h, d],
             device_id=at_users(xi, ring(zi, d, ZS), yi), device_id_type=MESH)
-        copy.start()
-        z_copies.append(copy)
+
+    for h in range(2):
+        for d in (4, 3, 5, 2, 6, 1, 7):
+            z_copy(h, d).start()
 
     for load in loads:
         load.wait()
     uft[...] = uf[...].T
 
-    for copy in z_copies:
-        copy.wait_recv()
-
     def x_copy(h, d):
         part = panel.at[xi, pl.ds(2 * h, 2)]
         return pltpu.make_async_remote_copy(
             src_ref=part, dst_ref=part, send_sem=xs_sem.at[h, d], recv_sem=xr_sem.at[h, d],
             device_id=at_users(ring(xi, d, XS), zi, yi), device_id_type=MESH)
 
-    for h in range(2):
+    def pass_on(h):
+        for d in range(1, ZS):
+            z_copy(h, d).wait_recv()
         for d in (1, 3, 2):
             x_copy(h, d).start()
+
+    pass_on(0)
 
     bits = jnp.left_shift(jnp.int32(1), lax.broadcasted_iota(jnp.int32, (1, 8, 128), 1))
 
@@ -137,7 +147,7 @@
 
     def chunk(q, h):
         pair = panel[q, pl.ds(2 * h, 2)].reshape(2 * QROWS, RANK)
-        half = lax.rem(q, 2)
+        lanes = pl.ds(pl.multiple_of(lax.rem(q, 2) * 128, 128), 128)
         p = lax.div(q, 2)
         for u in range(UTILES):
             span = pl.ds(u * TILE, TILE)
@@ -148,9 +158,9 @@
                 first = (2 * h + k) * SLOTS
                 slot = first + slots[first + 2 * u + p]
                 live = lives[first + 2 * u + p]
-                words = mask_v[half, slot] & live
+                words = mask_v[slot, :, lanes] & live
                 seen = (jnp.broadcast_to(words[:, None, :], (32, 8, 128)) & bits) != 0
-                gap = predicted[:, k * 128:(k + 1) * 128] - rat_v[half, slot].astype(F32)
+                gap = predicted[:, k * 128:(k + 1) * 128] - rat_v[slot, :, lanes].astype(F32)
                 kept = jnp.where(seen, gap.reshape(32, 8, 128), 0.0)
                 parts.append(kept.reshape(TILE, 128).astype(BF16))
             errors = jnp.concatenate(parts, axis=1)
@@ -167,6 +177,10 @@
                       jnp.where(k == 3, 0, jnp.where(k == 2, 3, 2 - k)))
         q = ring(xi, d, XS)
 
+        @pl.when(c == 1)
+        def _():
+            pass_on(1)
+
         @pl.when(d != 0)
         def _():
             x_copy(h, XS - d).wait_recv()
@@ -188,18 +202,13 @@
             send_sem=us_sem.at[d], recv_sem=ur_sem.at[d],
             device_id={"items": ring(it, d, ITEMS)}, device_id_type=MESH)
 
-    share = 2 * TILE
-    for d in (2, 3, 1):
-        rows = pl.ds(pl.multiple_of(ring(it, d, ITEMS) * share, share), share)
-        user_out[d] = user_sum[rows, :].astype(BF16)
-        u_copy(d).start()
-
     def zy_copy(h, d):
         return pltpu.make_async_remote_copy(
             src_ref=zy_out.at[h, d], dst_ref=zy_in.at[h, d],
             send_sem=zys_sem.at[h, d], recv_sem=zyr_sem.at[h, d],
             device_id={"users": xi * ZY + ring(zy, d, ZY)}, device_id_type=MESH)
 
+    share = 2 * TILE
     for h in range(2):
         for d in range(1, XS):
             g_copy(h, d).wait_recv()
@@ -210,6 +219,11 @@
             zy_out[h, d] = sums[h, :, rows, :].reshape(2 * ROWS, RANK).astype(BF16)
         for d in (8, 7, 9, 6, 10, 5, 11, 4, 12, 3, 13, 2, 14, 1, 15):
             zy_copy(h, d).start()
+        if h == 0:
+            for d in (2, 3, 1):
+                rows = pl.ds(pl.multiple_of(ring(it, d, ITEMS) * share, share), share)
+                user_out[d] = user_sum[rows, :].astype(BF16)
+                u_copy(d).start()
 
     my_share = pl.ds(pl.multiple_of(it * share, share), share)
     for d in range(1, ITEMS):
@@ -228,9 +242,9 @@
         new_items[0, pair] = 0.95 * items[0, pair] - step_rate * total.reshape(2, ROWS, RANK)
 
     y_copy.wait_send()
-    for copy in z_copies:
-        copy.wait_send()
     for h in range(2):
+        for d in range(1, ZS):
+            z_copy(h, d).wait_send()
         for d in range(1, XS):
             x_copy(h, d).wait_send()
             g_copy(h, d).wait_send()
@@ -241,7 +255,6 @@
 
 
 def shards(user_factors, item_factors, tile_user, tile_item, tile_count, ratings, mask):
-    smem = pl.BlockSpec(memory_space=pltpu.SMEM)
     vmem = pl.BlockSpec(memory_space=pltpu.VMEM)
     hbm = pl.BlockSpec(memory_space=pl.ANY)
     dma = pltpu.SemaphoreType.DMA
@@ -251,14 +264,18 @@
             jax.ShapeDtypeStruct(item_factors.shape, F32),
             jax.ShapeDtypeStruct((user_factors.shape[0] // ITEMS, RANK), F32),
         ),
-        in_specs=[smem, smem, smem, vmem, hbm, hbm, hbm],
+        in_specs=[hbm] * 7,
         out_specs=(vmem, vmem),
         scratch_shapes=[
+            pltpu.SMEM(tile_user.shape, jnp.int32),
+            pltpu.SMEM(tile_item.shape, jnp.int32),
+            pltpu.SMEM(tile_count.shape, jnp.int32),
+            pltpu.VMEM(item_factors.shape, F32),
             pltpu.SMEM((STEPS * SLOTS,), jnp.int32),
             pltpu.SMEM((STEPS * SLOTS,), jnp.int32),
             pltpu.SMEM((STEPS * SLOTS,), jnp.int32),
-            pltpu.VMEM((2, STEPS * SLOTS, TILE, 128), BF16),
-            pltpu.VMEM((2, STEPS * SLOTS, TILE // 8, 128), jnp.int32),
+            pltpu.VMEM((STEPS * SLOTS, TILE, TILE), BF16),
+            pltpu.VMEM((STEPS * SLOTS, TILE // 8, TILE), jnp.int32),
             pltpu.VMEM((UTILES * TILE, RANK), BF16),
             pltpu.VMEM((RANK, UTILES * TILE), BF16),
             pltpu.VMEM((XS, STEPS, QROWS, RANK), BF16),
@@ -274,12 +291,12 @@
             pltpu.VMEM((UTILES * TILE, RANK), F32),
             pltpu.VMEM((ITEMS, 2 * TILE, RANK), BF16),
             pltpu.VMEM((ITEMS, 2 * TILE, RANK), BF16),
-            dma((17,)), dma((2,)), dma((ZS,)), dma((ZS,)),
+            dma((13,)), dma((2,)), dma((2, ZS)), dma((2, ZS)),
             dma((2, XS)), dma((2, XS)), dma((2, XS)), dma((2, XS)),
             dma((2, ZY)), dma((2, ZY)), dma((ITEMS,)), dma((ITEMS,)),
         ],
         compiler_params=pltpu.CompilerParams(
-            collective_id=0, has_side_effects=True, vmem_limit_bytes=40 * 2**20),
+            collective_id=0, has_side_effects=True, vmem_limit_bytes=67043328),
         name="factor_step",
     )(tile_user, tile_item, tile_count, item_factors, user_factors, ratings, mask)
 

time: 51.9 us -> 43.7 us (0.84)
  the two profiles are of different devices: /device:TPU:6 before, /device:TPU:1 now
where the time goes in v2:
time: 43.7 us; the launch traced here: 43.5 us
  Pallas kernels  39.9 us (91%)
  local copies, waits for them, and re-layouts  2.99 us (7%)
  between operations  0.64 us (1%)
    pallas_call x1, Pallas kernels, shards(): pl.pallas_call(kernel, out_shape=(jax.ShapeDtypeStruct(item_factors.shape...  39.9 us
    unnamed x2, local copies, waits for them, and re-layouts  2.99 us

profile of v2, /device:TPU:1, one launch (start us, length us, event | category | flops | bytes accessed | tf_op | source)
XLA Modules:
  0.0 43.5 jit_solution(14778795362269039007)
XLA Ops:
  0.6 39.9 %factor_step.1 = (f32[1,4,8,128]{3,2,1,0:T(8,128)}, f32[512,128]{1,0:T(8,128)}) custom-call(s32[1,1,4,16]{3,2,1,0:T(4,128)} %tile_user_hbm.1, s32[1,1,4,16]{3,2,1,0:T(4,128)} %tile_item_hbm.1, s32[1,1,4]{2,1,0:T(1,128)} %tile_count_hbm.1, f32[1,4,8,128]{3,2,1,0:T(8,128)} %items_hbm.1, bf16[2048,128]{1,0:T(8,128)(2,1)} %factors.1, ...), custom_call_target="tpu_custom_call" | custom-call | tf_op jit(solution)/shard_map/factor_step/pallas_call | solution.py:261
  40.5 1.3 %copy.11 = f32[1,4,8,128]{3,2,1,0:T(8,128)} copy(f32[1,4,8,128]{3,2,1,0:T(8,128)} %get-tuple-element.4) | data formatting | bytes 32768
  41.8 1.7 %copy.12 = f32[512,128]{1,0:T(8,128)} copy(f32[512,128]{1,0:T(8,128)} %get-tuple-element.5) | data formatting | bytes 524288

commit v3 on v2

--- a/solution.py
+++ b/solution.py
@@ -27,7 +27,7 @@
     new_items, user_grad,
     tile_user, tile_item, tile_count, items,
     slots, lives, cells, rat_v, mask_v, uf, uft, panel, other, err, gacc,
-    own_grad, grad_out, grad_in, sums, zy_out, zy_in, user_sum, user_out, user_in,
+    own_grad, grad_out, grad_in, sums, zy_out, zy_in, user_part, user_out, user_in,
     load_sem, y_sem, zs_sem, zr_sem, xs_sem, xr_sem, gs_sem, gr_sem,
     zys_sem, zyr_sem, us_sem, ur_sem,
 ):
@@ -37,6 +37,10 @@
     zy = lax.rem(me, ZY)
     zi = lax.div(zy, YS)
     yi = lax.rem(zy, YS)
+
+    twin = it + 1 - 2 * lax.rem(it, 2)
+    across = lax.rem(it + 2, ITEMS)
+    far = lax.rem(twin + 2, ITEMS)
 
     def at_users(x, z, y):
         return {"users": x * ZY + z * YS + y}
@@ -66,8 +70,8 @@
     for d in range(1, XS):
         pl.semaphore_signal(barrier, inc=1, device_id={"users": ring(xi, d, XS) * ZY + zy}, device_id_type=MESH)
         greeted += 1
-    for d in range(1, ITEMS):
-        pl.semaphore_signal(barrier, inc=1, device_id={"items": ring(it, d, ITEMS)}, device_id_type=MESH)
+    for partner in (twin, across):
+        pl.semaphore_signal(barrier, inc=1, device_id={"items": partner}, device_id_type=MESH)
         greeted += 1
     for load in tables + loads:
         load.start()
@@ -92,8 +96,6 @@
         slots[idx] = slot
         lives[idx] = live
 
-    user_sum[...] = jnp.zeros_like(user_sum)
-
     pl.semaphore_wait(barrier, greeted)
 
     y_copy = pltpu.make_async_remote_copy(
@@ -147,6 +149,7 @@
 
     def chunk(q, h):
         pair = panel[q, pl.ds(2 * h, 2)].reshape(2 * QROWS, RANK)
+        columns = pl.ds(pl.multiple_of((2 * q + h) * 2 * QROWS, 2 * QROWS), 2 * QROWS)
         lanes = pl.ds(pl.multiple_of(lax.rem(q, 2) * 128, 128), 128)
         p = lax.div(q, 2)
         for u in range(UTILES):
@@ -163,18 +166,14 @@
                 gap = predicted[:, k * 128:(k + 1) * 128] - rat_v[slot, :, lanes].astype(F32)
                 kept = jnp.where(seen, gap.reshape(32, 8, 128), 0.0)
                 parts.append(kept.reshape(TILE, 128).astype(BF16))
-            errors = jnp.concatenate(parts, axis=1)
-            err[span, :] = errors
-            user_sum[span, :] += jnp.dot(errors, pair, preferred_element_type=F32)
-        gacc[...] = jnp.dot(uft[...], err[...], preferred_element_type=F32)
+            err[span, columns] = jnp.concatenate(parts, axis=1)
+        gacc[...] = jnp.dot(uft[...], err[:, columns], preferred_element_type=F32)
         return gacc[...].T.reshape(2, QROWS, RANK)
 
     @pl.loop(0, 8)
     def _(c):
-        h = lax.div(c, 4)
-        k = lax.rem(c, 4)
-        d = jnp.where(h == 0, jnp.where(k == 3, 2, jnp.where(k == 2, 3, k)),
-                      jnp.where(k == 3, 0, jnp.where(k == 2, 3, 2 - k)))
+        h = jnp.where(c < 2, c, jnp.where(c < 5, 0, 1))
+        d = jnp.where(c < 2, 0, jnp.where(c < 5, jnp.where(c == 2, 1, 6 - c), c - 4))
         q = ring(xi, d, XS)
 
         @pl.when(c == 1)
@@ -196,20 +195,13 @@
             grad_out[h, d] = grad.astype(BF16)
             g_copy(h, d).start()
 
-    def u_copy(d):
-        return pltpu.make_async_remote_copy(
-            src_ref=user_out.at[d], dst_ref=user_in.at[d],
-            send_sem=us_sem.at[d], recv_sem=ur_sem.at[d],
-            device_id={"items": ring(it, d, ITEMS)}, device_id_type=MESH)
-
     def zy_copy(h, d):
         return pltpu.make_async_remote_copy(
             src_ref=zy_out.at[h, d], dst_ref=zy_in.at[h, d],
             send_sem=zys_sem.at[h, d], recv_sem=zyr_sem.at[h, d],
             device_id={"users": xi * ZY + ring(zy, d, ZY)}, device_id_type=MESH)
 
-    share = 2 * TILE
-    for h in range(2):
+    def exchange(h):
         for d in range(1, XS):
             g_copy(h, d).wait_recv()
         sums[h] = own_grad[h] + (
@@ -219,17 +211,36 @@
             zy_out[h, d] = sums[h, :, rows, :].reshape(2 * ROWS, RANK).astype(BF16)
         for d in (8, 7, 9, 6, 10, 5, 11, 4, 12, 3, 13, 2, 14, 1, 15):
             zy_copy(h, d).start()
-        if h == 0:
-            for d in (2, 3, 1):
-                rows = pl.ds(pl.multiple_of(ring(it, d, ITEMS) * share, share), share)
-                user_out[d] = user_sum[rows, :].astype(BF16)
-                u_copy(d).start()
-
-    my_share = pl.ds(pl.multiple_of(it * share, share), share)
-    for d in range(1, ITEMS):
-        u_copy(d).wait_recv()
-    user_grad[...] = (user_sum[my_share, :] + (
-        user_in[1].astype(F32) + user_in[2].astype(F32) + user_in[3].astype(F32))) * (1.0 / 32.0)
+
+    share = 2 * TILE
+
+    def user_terms(owner):
+        rows = pl.ds(pl.multiple_of(owner * share, share), share)
+        every = panel[...].reshape(STEPS * XS * QROWS, RANK)
+        return jnp.dot(err[rows, :], every, preferred_element_type=F32)
+
+    def u_copy(k):
+        return pltpu.make_async_remote_copy(
+            src_ref=user_out.at[k], dst_ref=user_in.at[k],
+            send_sem=us_sem.at[k], recv_sem=ur_sem.at[k],
+            device_id={"items": across if k == 2 else twin}, device_id_type=MESH)
+
+    user_out[0] = user_terms(far).astype(BF16)
+    u_copy(0).start()
+    user_out[1] = user_terms(twin).astype(BF16)
+    u_copy(1).start()
+    exchange(0)
+    user_part[0] = user_terms(across)
+    user_part[1] = user_terms(it)
+    exchange(1)
+    u_copy(0).wait_recv()
+    user_out[2] = (user_part[0] + user_in[0].astype(F32)).astype(BF16)
+    u_copy(2).start()
+
+    u_copy(1).wait_recv()
+    user_part[1] = user_part[1] + user_in[1].astype(F32)
+    u_copy(2).wait_recv()
+    user_grad[...] = (user_part[1] + user_in[2].astype(F32)) * (1.0 / 32.0)
 
     step_rate = 8.0 / math.sqrt(TILE * XS * ZY)
     mine_rows = pl.ds(pl.multiple_of(zy * ROWS, ROWS), ROWS)
@@ -250,14 +261,15 @@
             g_copy(h, d).wait_send()
         for d in range(1, ZY):
             zy_copy(h, d).wait_send()
-    for d in range(1, ITEMS):
-        u_copy(d).wait_send()
+    for k in range(3):
+        u_copy(k).wait_send()
 
 
 def shards(user_factors, item_factors, tile_user, tile_item, tile_count, ratings, mask):
     vmem = pl.BlockSpec(memory_space=pltpu.VMEM)
     hbm = pl.BlockSpec(memory_space=pl.ANY)
     dma = pltpu.SemaphoreType.DMA
+    operands = (tile_user, tile_item, tile_count, item_factors, user_factors, ratings, mask)
     return pl.pallas_call(
         kernel,
         out_shape=(
@@ -280,7 +292,7 @@
             pltpu.VMEM((RANK, UTILES * TILE), BF16),
             pltpu.VMEM((XS, STEPS, QROWS, RANK), BF16),
             pltpu.VMEM((STEPS, ROWS, RANK), F32),
-            pltpu.VMEM((UTILES * TILE, 2 * QROWS), BF16),
+            pltpu.VMEM((UTILES * TILE, STEPS * XS * QROWS), BF16),
             pltpu.VMEM((RANK, 2 * QROWS), F32),
             pltpu.VMEM((2, 2, QROWS, RANK), F32),
             pltpu.VMEM((2, XS, 2, QROWS, RANK), BF16),
@@ -288,17 +300,17 @@
             pltpu.VMEM((2, 2, QROWS, RANK), F32),
             pltpu.VMEM((2, ZY, 2 * ROWS, RANK), BF16),
             pltpu.VMEM((2, ZY, 2 * ROWS, RANK), BF16),
-            pltpu.VMEM((UTILES * TILE, RANK), F32),
-            pltpu.VMEM((ITEMS, 2 * TILE, RANK), BF16),
-            pltpu.VMEM((ITEMS, 2 * TILE, RANK), BF16),
+            pltpu.VMEM((2, 2 * TILE, RANK), F32),
+            pltpu.VMEM((3, 2 * TILE, RANK), BF16),
+            pltpu.VMEM((3, 2 * TILE, RANK), BF16),
             dma((13,)), dma((2,)), dma((2, ZS)), dma((2, ZS)),
             dma((2, XS)), dma((2, XS)), dma((2, XS)), dma((2, XS)),
-            dma((2, ZY)), dma((2, ZY)), dma((ITEMS,)), dma((ITEMS,)),
+            dma((2, ZY)), dma((2, ZY)), dma((3,)), dma((3,)),
         ],
         compiler_params=pltpu.CompilerParams(
-            collective_id=0, has_side_effects=True, vmem_limit_bytes=67043328),
+            collective_id=0, has_side_effects=True, vmem_limit_bytes=48 * 2**20),
         name="factor_step",
-    )(tile_user, tile_item, tile_count, item_factors, user_factors, ratings, mask)
+    )(*(pltpu.with_memory_space_constraint(operand, pltpu.HBM) for operand in operands))
 
 
 def solution(mesh):

time: 43.7 us -> 40.8 us (0.934)
  the two profiles are of different devices: /device:TPU:1 before, /device:TPU:8 now
where the time goes in v3:
time: 40.8 us; the launch traced here: 40.5 us
  Pallas kernels  38.6 us (95%)
  local copies, waits for them, and re-layouts  1.31 us (3%)
  between operations  0.64 us (2%)
    pallas_call x1, Pallas kernels, shards(): pl.pallas_call(kernel, out_shape=(jax.ShapeDtypeStruct(item_factors.shape...  38.6 us
    unnamed x2, local copies, waits for them, and re-layouts  1.31 us

profile of v3, /device:TPU:8, one launch (start us, length us, event | category | flops | bytes accessed | tf_op | source)
XLA Modules:
  0.0 40.5 jit_solution(4165079581964623244)
XLA Ops:
  0.6 38.6 %factor_step.1 = (f32[1,4,8,128]{3,2,1,0:T(8,128)S(1)}, f32[512,128]{1,0:T(8,128)S(1)}) custom-call(s32[1,1,4,16]{3,2,1,0:T(4,128)} %tile_user_hbm.1, s32[1,1,4,16]{3,2,1,0:T(4,128)} %tile_item_hbm.1, s32[1,1,4]{2,1,0:T(1,128)} %tile_count_hbm.1, f32[1,4,8,128]{3,2,1,0:T(8,128)} %items_hbm.1, bf16[2048,128]{1,0:T(8,128)(2,1)} %factors.1, ...), custom_call_target="tpu_custom_call" | custom-call | tf_op jit(solution)/shard_map/factor_step/pallas_call | solution.py:273
  39.2 0.6 %copy.11 = f32[1,4,8,128]{3,2,1,0:T(8,128)} copy(f32[1,4,8,128]{3,2,1,0:T(8,128)S(1)} %get-tuple-element.4) | data formatting | bytes 32768
  39.8 0.7 %copy.12 = f32[512,128]{1,0:T(8,128)} copy(f32[512,128]{1,0:T(8,128)S(1)} %get-tuple-element.5) | data formatting | bytes 524288
